TPU v7x, 1024 devices: a whole 8x8x8 slice. The times are simulated.
1024 devices in a mesh: row: 8 (over x_lo, core), col: 128 (over x_hi, y, z).
Axes of the slice: x: 8 (x_hi: 2, x_lo: 4; x = x_hi * 4 + x_lo), y: 8, z: 8, core: 2. Of those that a mesh axis runs over, the one named last changes fastest.
Arguments:
- blocks: float32 [8, 128, 4, 128, 128], P('row', 'col')
- block_rows: int32 [8, 128, 4], P('row', 'col'), may hold values from 0 to 31, as said below
- block_cols: int32 [8, 128, 4], P('row', 'col'), may hold values from 0 to 7
- counts: int32 [8, 128], P('row', 'col'), may hold values from 2 to 4, as said below
- x_prev: float32 [131072], P('col'), may hold values from 0 to 1
- y_prev: float32 [32768], P('row'), may hold values from -6 to 6
- cost: float32 [131072], P('col'), may hold values from -6 to 6
- rhs: float32 [32768], P('row'), may hold values from -6 to 6
- upper: float32 [131072], P('col'), may hold values from 0.5 to 4
- steps: float32 [2], replicated, may hold values from 0.1 to 0.4
Outputs:
- x_new: float32 [131072], P('col')
- y_new: float32 [32768], P('row')
- stats: float32 [3], replicated
Inputs may be any that keep to these rules, and one draw needn't show every extreme that they name: `block_rows`: pairs of block row and block column may repeat within a device. `counts`: stored blocks at positions from the count on are padding and are not part of the matrix; some device holds 4 live blocks in every draw.
All inputs are finite; a program needn't handle non-finite values.
Results may differ from a plain program's by a relative error of at most 0.00011.
Values sent between devices are 32-bit elements; how exact they have to be, the bound alone decides.
A program may use at most 32 MiB of HBM per device.

v0:
```python
import jax
import jax.numpy as jnp
from jax import lax
from jax.sharding import PartitionSpec as P


def shards(blocks, block_rows, block_cols, counts, x_prev, y_prev, cost, rhs, upper, steps):
    flat = blocks[0, 0]
    nbd = flat.shape[0]
    bsz = flat.shape[1]
    brow = block_rows[0, 0]
    bcol = block_cols[0, 0]
    live = (jnp.arange(nbd, dtype=jnp.int32) < counts[0, 0]).astype(jnp.float32)
    nrows = y_prev.shape[0]
    ncols = x_prev.shape[0]
    rblocks = nrows // bsz
    cblocks = ncols // bsz
    row_hot = (brow[:, None] == jnp.arange(rblocks, dtype=jnp.int32)[None, :]).astype(jnp.float32)
    col_hot = (bcol[:, None] == jnp.arange(cblocks, dtype=jnp.int32)[None, :]).astype(jnp.float32)
    row_live = row_hot * live[:, None]
    col_live = col_hot * live[:, None]
    rpeak = jnp.max(jnp.abs(flat), axis=2)
    cpeak = jnp.max(jnp.abs(flat), axis=1)
    rpeak = jnp.max(row_live[:, :, None] * rpeak[:, None, :], axis=0).reshape(-1)
    cpeak = jnp.max(col_live[:, :, None] * cpeak[:, None, :], axis=0).reshape(-1)
    rowmax = lax.pmax(rpeak, "col")
    colmax = lax.pmax(cpeak, "row")
    row_scale = 1.0 / jnp.sqrt(jnp.maximum(rowmax, 0.5))
    col_scale = 1.0 / jnp.sqrt(jnp.maximum(colmax, 0.5))

    def backward(vec):
        scaled = (vec * row_scale).reshape(rblocks, bsz)
        picked = jnp.einsum("kr,ri->ki", row_hot, scaled, precision=lax.Precision.HIGHEST)
        prod = jnp.einsum("kij,ki->kj", flat, picked, precision=lax.Precision.HIGHEST)
        partial_value = jnp.einsum(
            "kc,kj->cj", col_live, prod, precision=lax.Precision.HIGHEST
        ).reshape(-1)
        return lax.psum(partial_value, "row") * col_scale

    cost_s = col_scale * cost
    rhs_s = row_scale * rhs
    upper_s = upper / col_scale
    eta = steps[0]
    omega = steps[1]
    tau = eta / omega
    sigma = eta * omega
    grad = cost_s - backward(y_prev)
    x_new = jnp.clip(x_prev - tau * grad, 0.0, upper_s)
    delta_x = x_new - x_prev
    vecs = jnp.stack([x_new, delta_x])
    count = vecs.shape[0]
    scaled = (vecs * col_scale[None, :]).reshape(count, cblocks, bsz)
    picked = jnp.einsum("kc,vcj->vkj", col_hot, scaled, precision=lax.Precision.HIGHEST)
    prod = jnp.einsum("kij,vkj->kvi", flat, picked, precision=lax.Precision.HIGHEST)
    summed = jnp.einsum("kr,kvi->vri", row_live, prod, precision=lax.Precision.HIGHEST)
    partial_value = summed.reshape(count, nrows)
    share = nrows // lax.axis_size("col")
    start = lax.axis_index("col") * share

    def piece(vec):
        return lax.dynamic_slice_in_dim(vec, start, share)

    summed = lax.psum(partial_value, "col")
    ax_new = summed[0] * row_scale
    adx = summed[1] * row_scale
    y_new = y_prev + sigma * (rhs_s - ax_new - adx)
    rhs_piece = piece(rhs_s)
    y_new_piece = piece(y_new)
    delta_y = y_new_piece - piece(y_prev)
    adx_piece = piece(adx)
    resid = rhs_piece - piece(ax_new)
    dual_terms = jnp.stack(
        [
            jnp.sum(delta_y * delta_y),
            jnp.sum(adx_piece * adx_piece),
            jnp.sum(resid * resid),
            jnp.sum(rhs_piece * y_new_piece),
        ]
    )
    dual_total = lax.psum(dual_terms, ("row", "col"))
    reduced = cost_s - backward(y_new)
    primal_terms = jnp.stack(
        [
            jnp.sum(delta_x * delta_x),
            jnp.sum(cost_s * x_new),
            jnp.sum(upper_s * jnp.maximum(-reduced, 0.0)),
        ]
    )
    primal_total = lax.psum(primal_terms, "col")
    total_rows = nrows * lax.axis_size("row")
    total_cols = ncols * lax.axis_size("col")
    movement = 0.5 * omega * primal_total[0] + 0.5 / omega * dual_total[0]
    stats = jnp.stack(
        [
            jnp.sqrt(dual_total[2] / total_rows),
            (primal_total[1] - dual_total[3] + primal_total[2]) / total_cols,
            movement / jnp.sqrt(dual_total[1] * dual_total[0] + 1e-06),
        ]
    )
    return (x_new, y_new, stats)


def solution(mesh):
    placed = (
        P("row", "col", None, None, None),
        P("row", "col", None),
        P("row", "col", None),
        P("row", "col"),
        P("col"),
        P("row"),
        P("col"),
        P("row"),
        P("col"),
        P(),
    )
    return jax.shard_map(
        shards, mesh=mesh, in_specs=placed, out_specs=(P("col"), P("row"), P()), check_vma=False
    )
```

profile of v0, /device:TPU:8, one launch (start us, length us, event | category | flops | bytes accessed | tf_op | source)
XLA Modules:
  0.0 2338.4 jit_solution(9527959636222240962)
XLA Ops:
  0.6 0.0 copy-start
  1.3 0.7 fusion.27
  2.1 1.1 fusion.7
  3.2 0.1 multiply_reduce_fusion
  3.3 0.0 copy-start.2
  3.3 0.0 copy-start.10
  3.3 873.2 %pmax.15 = f32[4096]{0:T(1024)S(1)} all-reduce(f32[4096]{0:T(1024)S(1)} %bitcast.74), channel_id=1, replica_groups=mesh['row'=8,'col'=128] {'col'}, use_global_device_ids=true, to_apply=%region_5.0 | all-reduce | flops 4096 | bytes 32768 | tf_op jit(solution)/shard_map/pmax | solution.py:26
  876.5 0.0 copy-done.2
  876.5 0.0 copy-done.10
  876.5 0.2 fusion.10
  876.6 0.0 copy-done
  876.6 0.3 fusion.4
  877.0 0.0 copy-start.8
  877.0 0.7 copy-done.8
  877.6 0.3 convolution_bitcast_fusion.3
  877.9 13.6 psum.35
  891.5 0.1 fusion.29
  891.5 0.1 multiply_reduce_fusion.1
  891.6 0.0 copy-start.9
  891.6 0.0 copy-start.7
  891.6 13.7 pmax.14
  905.4 0.0 copy-done.9
  905.4 0.0 copy-start.6
  905.4 0.6 fusion.54
  906.0 0.0 copy-start.5
  907.3 0.0 copy-done.7
  907.3 0.0 copy-done.6
  907.3 0.0 copy-done.5
  907.4 0.0 copy-start.1
  907.4 0.3 convolution_bitcast_fusion
  907.7 0.1 copy.15
  907.8 0.5 fusion.2
  908.3 0.3 convolution_bitcast_fusion.1
  908.7 854.3 %psum.36 = f32[2,4096]{1,0:T(2,128)S(1)} all-reduce(f32[2,4096]{1,0:T(2,128)S(1)} %bitcast.73), channel_id=1, replica_groups=mesh['row'=8,'col'=128] {'col'}, use_global_device_ids=true, to_apply=%region_7.8 | all-reduce | flops 8192 | bytes 65536 | tf_op jit(solution)/shard_map/psum | solution.py:63
  1763.0 0.0 copy-start.4
  1764.3 0.0 copy-done.4
  1764.3 0.0 copy-start.3
  1764.3 0.8 multiply_reduce_fusion.8
  1765.1 2.6 pad_maximum_fusion
  1767.7 111.2 %psum.37 = f32[4]{0:T(128)S(1)} all-reduce(f32[4]{0:T(128)S(1)} %pad_maximum_fusion), channel_id=1, replica_groups=mesh['row'=8,'col'=128] {'row','col'}, use_global_device_ids=true, to_apply=%region_12.13 | all-reduce | flops 4 | bytes 32 | tf_op jit(solution)/shard_map/psum | solution.py:80
  1878.8 0.7 fusion.52
  1879.5 0.0 copy-done.3
  1879.5 0.2 fusion.8
  1879.7 0.3 fusion
  1880.0 0.3 convolution_bitcast_fusion.2
  1880.3 14.7 psum.38
  1895.0 0.0 copy-done.1
  1895.0 0.6 multiply_reduce_fusion.3
  1895.7 1.9 pad_maximum_fusion.1
  1897.5 433.3 %psum.39 = f32[3]{0:T(128)S(1)} all-reduce(f32[3]{0:T(128)S(1)} %pad_maximum_fusion.1), channel_id=1, replica_groups=mesh['row'=8,'col'=128] {'col'}, use_global_device_ids=true, to_apply=%region_17.18 | all-reduce | flops 3 | bytes 24 | tf_op jit(solution)/shard_map/psum | solution.py:89
  2330.9 0.6 fusion.53
  2337.8 0.6 pad_maximum_fusion.2
  (5 shorter events, 0.1 us)
Async XLA Ops:
  0.6 876.0 %copy-start = (f32[1,1,4,128,128]{4,3,2,1,0:T(8,128)S(1)}, f32[1,1,4,128,128]{4,3,2,1,0:T(8,128)}, u32[]{:S(2)}) copy-start(f32[1,1,4,128,128]{4,3,2,1,0:T(8,128)} %param.10) | copy-start | bytes 786436
  3.3 873.2 %copy-start.2 = (f32[4096]{0:T(1024)S(1)}, f32[4096]{0:T(1024)}, u32[]{:S(2)}) copy-start(f32[4096]{0:T(1024)} %param.15) | copy-start | bytes 49156
  3.3 873.2 %copy-start.10 = (s32[1,1,4]{2,1,0:T(1,128)S(1)}, s32[1,1,4]{2,1,0:T(1,128)}, u32[]{:S(2)}) copy-start(s32[1,1,4]{2,1,0:T(1,128)} %param.11) | copy-start | bytes 52
  877.0 0.7 copy-start.8
  891.6 13.7 copy-start.9
  891.6 15.7 copy-start.7
  905.4 2.0 copy-start.6
  906.0 1.4 copy-start.5
  907.4 987.7 %copy-start.1 = (f32[1024]{0:T(1024)}, f32[1024]{0:T(1024)S(1)}, u32[]{:S(2)}) copy-start(f32[1024]{0:T(1024)S(1)} %get-tuple-element.16) | copy-start | bytes 12292
  1763.0 1.3 copy-start.4
  1764.3 115.2 %copy-start.3 = (f32[4096]{0:T(1024)}, f32[4096]{0:T(1024)S(1)}, u32[]{:S(2)}) copy-start(f32[4096]{0:T(1024)S(1)} %get-tuple-element.11) | copy-start | bytes 49156
where the time goes:
time: 2340 us
  blocking collectives  2310 us (99%)
    pmax x1, blocking collectives, shards(): rowmax = lax.pmax(rpeak, 'col')  873 us
    psum x1, blocking collectives, shards(): summed = lax.psum(partial_value, 'col')  854 us
    psum x1, blocking collectives, shards(): primal_total = lax.psum(primal_terms, 'col')  433 us
    psum x1, blocking collectives, shards(): dual_total = lax.psum(dual_terms, ('row', 'col'))  111 us

commit v1 on v0

v1 whole, which is shorter than its diff:
```python
import functools

import jax
import jax.numpy as jnp
from jax import lax
from jax.experimental import pallas as pl
from jax.experimental.pallas import tpu as pltpu
from jax.sharding import PartitionSpec as P

MESH = pl.DeviceIdType.MESH
LANES = 128
COL_GRID = {128: (2, 8, 8), 8: (2, 2, 2)}
STOP = 99


def far_first(n):
    return sorted(range(1, n), key=lambda d: -min(d, n - d))


def total(terms, op):
    acc = terms[0]
    for term in terms[1:]:
        acc = op(acc, term)
    return acc


def body(
    grid, nrow, nbd,
    brow_ref, bcol_ref, count_ref, steps_ref, blocks_ref, x_ref, y_ref, cost_ref, rhs_ref, upper_ref,
    x_out, y_out, stats_out,
    flip_ref, scaled_ref, vec_ref,
    max_send, max_y, max_z, max_x, max_all, cmax_buf,
    part_buf, fwd_send, fwd_y, fwd_z, fwd_x, fwd_all, dual_buf, back_buf, sum_y, sum_z, sum_x,
    send_sems, recv_sems,
):
    nx, ny, nz = grid
    rb = y_ref.shape[0]
    cb = x_ref.shape[0]
    share = rb // ny
    row = lax.axis_index("row")
    col = lax.axis_index("col")
    xh = col // (ny * nz)
    yi = (col // nz) % ny
    zi = col % nz

    def y_peer(d):
        other = (yi + d) % ny
        return (row, (xh * ny + other) * nz + zi), other

    def z_peer(d):
        other = (zi + d) % nz
        return (row, (xh * ny + yi) * nz + other), other

    def x_peer(d):
        other = (xh + d) % nx
        return (row, (other * ny + yi) * nz + zi), other

    def r_peer(d):
        other = (row + d) % nrow
        return (other, col), other

    lines = {"y": (y_peer, yi, ny), "z": (z_peer, zi, nz), "x": (x_peer, xh, nx), "r": (r_peer, row, nrow)}
    barrier = pltpu.get_barrier_semaphore()
    greeted = 0
    for peer, _, n in lines.values():
        for d in far_first(n):
            pl.semaphore_signal(barrier, inc=1, device_id=peer(d)[0], device_id_type=MESH)
            greeted += 1

    used = [0]
    pending = []

    def send(axis, buf, source=None):
        peer, me, n = lines[axis]
        base = used[0]
        used[0] += n - 1
        for d in far_first(n):
            device, other = peer(d)
            copy = pltpu.make_async_remote_copy(
                src_ref=buf.at[me] if source is None else source(other),
                dst_ref=buf.at[me],
                send_sem=send_sems.at[base + d - 1],
                recv_sem=recv_sems.at[base + d - 1],
                device_id=device,
                device_id_type=MESH,
            )
            copy.start()
            pending.append(copy)

        def arrive():
            for d in far_first(n)[::-1]:
                device, other = peer(n - d)
                pltpu.make_async_remote_copy(
                    src_ref=buf.at[other],
                    dst_ref=buf.at[other],
                    send_sem=send_sems.at[base + d - 1],
                    recv_sem=recv_sems.at[base + d - 1],
                    device_id=device,
                    device_id_type=MESH,
                ).wait_recv()

        return arrive

    def whole(buf, op):
        return total([buf[i] for i in range(buf.shape[0])], op)

    count = count_ref[0]
    rows = [jnp.where(k < count, brow_ref[k], -1) for k in range(nbd)]
    cols = [jnp.where(k < count, bcol_ref[k], -1) for k in range(nbd)]
    share_at = lax.broadcasted_iota(jnp.int32, (share, LANES), 0)
    cb_at = lax.broadcasted_iota(jnp.int32, (cb, LANES), 0)

    col_peak = jnp.zeros((cb, LANES), jnp.float32)
    row_peaks = []
    for k in range(nbd):
        block = blocks_ref[k]
        flip = block.T
        flip_ref[k] = flip
        row_peaks.append(jnp.max(jnp.abs(flip), axis=0, keepdims=True))
        peak = jnp.max(jnp.abs(block), axis=0, keepdims=True)
        col_peak = jnp.maximum(col_peak, jnp.where(cb_at == cols[k], peak, 0.0))
    for j in range(ny):
        max_send[j] = total(
            [jnp.where(share_at + j * share == rows[k], row_peaks[k], 0.0) for k in range(nbd)], jnp.maximum
        )
    cmax_buf[row] = col_peak
    max_y[yi] = max_send[yi]
    pl.semaphore_wait(barrier, greeted)
    if STOP <= 0:
        return

    arrive_y = send("y", max_y, lambda other: max_send.at[other])
    arrive_c = send("r", cmax_buf)
    arrive_y()
    max_z[zi] = whole(max_y, jnp.maximum)
    arrive = send("z", max_z)
    arrive_c()
    col_scale = 1.0 / jnp.sqrt(jnp.maximum(whole(cmax_buf, jnp.maximum), 0.5))
    arrive()
    max_x[xh] = whole(max_z, jnp.maximum)
    send("x", max_x)()
    row_scale = 1.0 / jnp.sqrt(jnp.maximum(whole(max_x, jnp.maximum), 0.5))
    max_all[yi] = row_scale
    send("y", max_all)()

    def picked(read):
        got = jnp.concatenate([read(brow_ref[k]) for k in range(nbd)] * (8 // nbd), axis=0)
        return got.T

    def scale_of(at):
        return max_all[at // share, pl.ds(at % share, 1), :]

    def backward(read):
        vec = picked(lambda at: read(at) * scale_of(at))
        out = jnp.zeros((cb, LANES), jnp.float32)
        for k in range(nbd):
            prod = jnp.sum(blocks_ref[k] * vec[:, k : k + 1], axis=0, keepdims=True)
            out = out + jnp.where(cb_at == cols[k], prod, 0.0)
        return out

    eta = steps_ref[0]
    omega = steps_ref[1]
    omega_v = jnp.full((1, 1), omega)
    tau = eta / omega_v
    sigma = eta * omega

    part_buf[row] = backward(lambda at: y_ref[pl.ds(at, 1), :])
    send("r", part_buf)()
    cost_s = col_scale * cost_ref[...]
    upper_s = upper_ref[...] / col_scale
    x_prev = x_ref[...]
    grad = cost_s - whole(part_buf, jnp.add) * col_scale
    x_new = jnp.clip(x_prev - tau * grad, 0.0, upper_s)
    delta_x = x_new - x_prev
    x_out[...] = x_new
    vec_ref[0] = x_new * col_scale
    vec_ref[1] = delta_x * col_scale

    vecs = jnp.concatenate(
        [vec_ref[v, pl.ds(bcol_ref[k], 1), :] for v in range(2) for k in range(nbd)], axis=0
    ).T
    pair_at = lax.broadcasted_iota(jnp.int32, (2 * share, LANES), 0)
    pair_row = pair_at % share
    prods = []
    for k in range(nbd):
        flip = flip_ref[k]
        ax = jnp.sum(flip * vecs[:, k : k + 1], axis=0, keepdims=True)
        adx = jnp.sum(flip * vecs[:, nbd + k : nbd + k + 1], axis=0, keepdims=True)
        prods.append(jnp.where(pair_at < share, ax, adx))
    for j in range(ny):
        fwd_send[j] = total(
            [jnp.where(pair_row + j * share == rows[k], prods[k], 0.0) for k in range(nbd)], jnp.add
        )
    fwd_y[yi] = fwd_send[yi]
    send("y", fwd_y, lambda other: fwd_send.at[other])()
    fwd_z[zi] = whole(fwd_y, jnp.add)
    send("z", fwd_z)()
    fwd_x[xh] = whole(fwd_z, jnp.add)
    send("x", fwd_x)()
    pair = whole(fwd_x, jnp.add)
    ax = pair[:share] * row_scale
    adx = pair[share:] * row_scale
    start = pl.multiple_of(yi * share, share)
    rhs_s = row_scale * rhs_ref[yi]
    y_prev = y_ref[pl.ds(start, share), :]
    y_new = y_prev + sigma * (rhs_s - ax - adx)
    delta_y = y_new - y_prev
    resid = rhs_s - ax
    fwd_all[yi, :share] = y_new
    for at, term in enumerate((delta_y * delta_y, adx * adx, resid * resid, rhs_s * y_new)):
        fwd_all[yi, share + at : share + at + 1] = jnp.sum(term, axis=0, keepdims=True)
    send("y", fwd_all)()
    dual_buf[row] = total([fwd_all[j, share : share + 4] for j in range(ny)], jnp.add)
    arrive_dual = send("r", dual_buf)
    for j in range(ny):
        y_out[j * share : (j + 1) * share] = fwd_all[j, :share]
    back_buf[row] = backward(lambda at: fwd_all[at // share, pl.ds(at % share, 1), :])
    arrive = send("r", back_buf)
    arrive_dual()
    dual = jnp.sum(whole(dual_buf, jnp.add), axis=1, keepdims=True)
    arrive()
    reduced = cost_s - whole(back_buf, jnp.add) * col_scale
    slot = lax.broadcasted_iota(jnp.int32, (8, LANES), 0)
    terms = [
        jnp.sum(term, axis=0, keepdims=True)
        for term in (delta_x * delta_x, cost_s * x_new, upper_s * jnp.maximum(-reduced, 0.0))
    ]
    sum_y[yi] = jnp.where(slot == 0, terms[0], jnp.where(slot == 1, terms[1], jnp.where(slot == 2, terms[2], 0.0)))
    send("y", sum_y)()
    sum_z[zi] = whole(sum_y, jnp.add)
    send("z", sum_z)()
    sum_x[xh] = whole(sum_z, jnp.add)
    send("x", sum_x)()
    primal = jnp.sum(whole(sum_x, jnp.add), axis=1, keepdims=True)
    dx2, cx, uneg = primal[0:1], primal[1:2], primal[2:3]
    dy2, adx2, res2, by = dual[0:1], dual[1:2], dual[2:3], dual[3:4]
    m = rb * LANES * nrow
    n = cb * LANES * nx * ny * nz
    movement = 0.5 * omega * dx2 + 0.5 / omega_v * dy2
    lane = lax.broadcasted_iota(jnp.int32, (1, LANES), 1)
    stats_out[...] = jnp.where(
        lane == 0,
        jnp.sqrt(res2 / m),
        jnp.where(lane == 1, (cx - by + uneg) / n, movement / jnp.sqrt(adx2 * dy2 + 1e-06)),
    )
    for copy in pending:
        copy.wait_send()


def shards(grid, nrow, blocks, block_rows, block_cols, counts, x_prev, y_prev, cost, rhs, upper, steps):
    nx, ny, nz = grid
    nbd, bsz = blocks.shape[2], blocks.shape[3]
    rb = y_prev.shape[0] // bsz
    cb = x_prev.shape[0] // bsz
    share = rb // ny
    copies = 4 * (ny - 1) + 3 * (nz - 1) + 3 * (nx - 1) + 4 * (nrow - 1) + (ny - 1)
    vmem = pl.BlockSpec(memory_space=pltpu.VMEM)
    smem = pl.BlockSpec(memory_space=pltpu.SMEM)
    f32 = jnp.float32

    def buf(n, rows):
        return pltpu.VMEM((n, rows, LANES), f32)

    x_new, y_new, stats = pl.pallas_call(
        functools.partial(body, grid, nrow, nbd),
        out_shape=(
            jax.ShapeDtypeStruct((cb, bsz), f32),
            jax.ShapeDtypeStruct((rb, bsz), f32),
            jax.ShapeDtypeStruct((1, LANES), f32),
        ),
        in_specs=[smem] * 4 + [vmem] * 6,
        out_specs=(vmem, vmem, vmem),
        scratch_shapes=[
            pltpu.VMEM((nbd, bsz, bsz), f32),
            buf(ny, share),
            buf(2, cb),
            buf(ny, share), buf(ny, share), buf(nz, share), buf(nx, share), buf(ny, share), buf(nrow, cb),
            buf(nrow, cb), buf(ny, 2 * share), buf(ny, 2 * share), buf(nz, 2 * share), buf(nx, 2 * share),
            buf(ny, 2 * share), buf(nrow, 4), buf(nrow, cb), buf(ny, 8), buf(nz, 8), buf(nx, 8),
            pltpu.SemaphoreType.DMA((copies,)),
            pltpu.SemaphoreType.DMA((copies,)),
        ],
        compiler_params=pltpu.CompilerParams(collective_id=0, has_side_effects=True),
        name="pdlp",
    )(
        block_rows.reshape(nbd),
        block_cols.reshape(nbd),
        counts.reshape(1),
        steps,
        blocks.reshape(nbd, bsz, bsz),
        x_prev.reshape(cb, bsz),
        y_prev.reshape(rb, bsz),
        cost.reshape(cb, bsz),
        rhs.reshape(ny, share, bsz),
        upper.reshape(cb, bsz),
    )
    return x_new.reshape(-1), y_new.reshape(-1), stats[0, :3]


def solution(mesh):
    placed = (
        P("row", "col", None, None, None),
        P("row", "col", None),
        P("row", "col", None),
        P("row", "col"),
        P("col"),
        P("row"),
        P("col"),
        P("row"),
        P("col"),
        P(),
    )
    return jax.shard_map(
        functools.partial(shards, COL_GRID[mesh.shape["col"]], mesh.shape["row"]),
        mesh=mesh,
        in_specs=placed,
        out_specs=(P("col"), P("row"), P()),
        check_vma=False,
    )
```

time: 2340 us -> 87.9 us (0.04)
  the two profiles are of different devices: /device:TPU:8 before, /device:TPU:1 now
where the time goes in v1:
time: 87.9 us; the launch traced here: 86.8 us
  Pallas kernels  82.4 us (94%)
  local copies, waits for them, and re-layouts  3.03 us (3%)
  between operations  1.3 us (1%)
    pallas_call x1, Pallas kernels, shards(): pl.pallas_call(functools.partial(body, grid, nrow, nbd), out_shape=(jax.S...  82.4 us
    unnamed x4, local copies, waits for them, and re-layouts  1.88 us

profile of v1, /device:TPU:1, one launch (start us, length us, event | category | flops | bytes accessed | tf_op | source)
XLA Modules:
  0.0 86.8 jit_solution(12463346054984777767)
XLA Ops:
  1.3 82.4 %pdlp.1 = (f32[8,128]{1,0:T(8,128)}, f32[32,128]{1,0:T(8,128)}, f32[1,128]{1,0:T(1,128)}) custom-call(s32[4]{0:T(128)} %bitcast.22, s32[4]{0:T(128)} %bitcast.23, s32[1]{0:T(128)} %bitcast.13.count_ref, f32[2]{0:T(128)} %steps_ref.1, f32[4,128,128]{2,1,0:T(8,128)} %bitcast.14, f32[8,128]{1,0:T(8,128)} %bitcast.18, f32[32,128]{1,0:T(8,128)} %bitcast.15, ...), custom_call_target="tpu_custom_call" | custom-call | tf_op jit(solution)/shard_map/pdlp/pallas_call | solution.py:264
  83.7 0.0 copy-start
  83.7 1.2 %slice_bitcast_fusion = f32[3]{0:T(128)} fusion(f32[1,128]{1,0:T(1,128)} %get-tuple-element.8), kind=kLoop, calls=%fused_computation | loop fusion | bytes 24 | tf_op jit(solution)/shard_map/squeeze | solution.py:297
  84.9 1.3 %copy.16 = f32[1024]{0:T(1024)} copy(f32[1024]{0:T(1024)} %bitcast.21) | data formatting | bytes 8192
  86.1 0.0 copy-done
  86.1 0.6 copy.17
Async XLA Ops:
  83.7 2.4 %copy-start = (f32[32,128]{1,0:T(8,128)S(1)}, f32[32,128]{1,0:T(8,128)}, u32[]{:S(2)}) copy-start(f32[32,128]{1,0:T(8,128)} %get-tuple-element.7) | copy-start | bytes 49156

commit v2 on v0

v2 whole, which is shorter than its diff:
```python
import functools

import jax
import jax.numpy as jnp
from jax import lax
from jax.experimental import pallas as pl
from jax.experimental.pallas import tpu as pltpu
from jax.sharding import PartitionSpec as P

MESH = pl.DeviceIdType.MESH
LANES = 128
NOWHERE = 1000.0
COL_GRID = {128: (2, 8, 8), 16: (2, 4, 2)}


def hops(d, n):
    return min(d, n - d)


def far_first(n):
    return sorted(range(1, n), key=lambda d: -hops(d, n))


def total(terms, op):
    acc = terms[0]
    for term in terms[1:]:
        acc = op(acc, term)
    return acc


def body(
    grid, nrow, nbd,
    brow_hbm, bcol_hbm, count_hbm, steps_hbm, blocks_hbm, x_hbm, y_hbm, cost_hbm, rhs_hbm, upper_hbm,
    x_out, y_out, stats_out,
    brow_ref, bcol_ref, count_ref, steps_ref, blocks_ref, x_ref, y_ref, cost_ref, rhs_ref, upper_ref,
    flip_ref, vec_ref, scale_ref, hot_ref,
    max_y, max_q, cmax_buf, part_buf, fwd_buf, dual_buf, back_buf, sum_buf,
    local_sems, send_sems, recv_sems, reached,
):
    nx, ny, nz = grid
    rb = y_ref.shape[0]
    cb = x_ref.shape[0]
    nq = nx * nz
    ncol = nq * ny
    qlanes = ny * 2 * nbd
    qper = LANES // qlanes
    row = lax.axis_index("row")
    col = lax.axis_index("col")
    xh = lax.div(col, ny * nz)
    yi = lax.rem(lax.div(col, nz), ny)
    zi = lax.rem(col, nz)
    xs = [lax.rem(xh + d, nx) for d in range(nx)]
    ys = [lax.rem(yi + d, ny) for d in range(ny)]
    zs = [lax.rem(zi + d, nz) for d in range(nz)]
    rs = [lax.rem(row + d, nrow) for d in range(nrow)]
    mirror = (nrow // 2 - 1 - lax.div(row, 2)) * 2 + lax.rem(row, 2)
    qi = xh * nz + zi
    slot = qi * ny + yi

    def col_device(d):
        dx, dy, dz = d
        return (row, (xs[dx] * ny + ys[dy]) * nz + zs[dz])

    def mirror_device(d):
        return (mirror if d[0] else row, col_device(d)[1])

    def row_device(d):
        return (rs[d], col)

    def ordered(offsets):
        cost = lambda d: (nx // 2) * 4 * d[0] + hops(d[1], ny) + hops(d[2], nz)
        return sorted(offsets, key=lambda d: -cost(d))

    line_y = [(0, d, 0) for d in far_first(ny)]
    line_z = [(0, 0, d) for d in far_first(nz)]
    plane = ordered([(a, 0, c) for a in range(nx) for c in range(nz) if a or c])
    everyone = ordered([(a, b, c) for a in range(nx) for b in range(ny) for c in range(nz) if a or b or c])
    line_r = far_first(nrow)

    barrier = pltpu.get_barrier_semaphore()
    near = [col_device(d) for d in line_y] + [row_device(d) for d in line_r]
    near += [col_device(d) for d in line_z] + [col_device((1, 0, 0))]
    for device in near:
        pl.semaphore_signal(barrier, inc=1, device_id=device, device_id_type=MESH)
    fetches = [
        pltpu.make_async_copy(src, dst, local_sems.at[i])
        for i, (src, dst) in enumerate(
            (
                (blocks_hbm, blocks_ref), (brow_hbm, brow_ref), (bcol_hbm, bcol_ref), (count_hbm, count_ref),
                (y_hbm, y_ref), (x_hbm, x_ref), (cost_hbm, cost_ref), (rhs_hbm, rhs_ref), (upper_hbm, upper_ref),
                (steps_hbm, steps_ref),
            )
        )
    ]
    for copy in fetches:
        copy.start()
    finish = []

    def send(at, peers, buf, me):
        for device in peers:
            pltpu.make_async_remote_copy(
                src_ref=buf.at[me],
                dst_ref=buf.at[me],
                send_sem=send_sems.at[at],
                recv_sem=recv_sems.at[at],
                device_id=device,
                device_id_type=MESH,
            ).start()
        theirs = buf.at[pl.ds(0, len(peers))]
        finish.append(pltpu.make_async_copy(theirs, theirs, send_sems.at[at]))
        return pltpu.make_async_copy(theirs, theirs, recv_sems.at[at]).wait

    def whole(buf, op):
        return total([buf[i] for i in range(buf.shape[0])], op)

    for copy in fetches[:4]:
        copy.wait()
    count = count_ref[0, 0]
    brow = [brow_ref[0, 0, k] for k in range(nbd)]
    bcol = [bcol_ref[0, 0, k] for k in range(nbd)]
    rows = [jnp.where(k < count, brow[k].astype(jnp.float32), NOWHERE) for k in range(nbd)]
    cols = [jnp.where(k < count, bcol[k], -1) for k in range(nbd)]
    tile_at = lax.broadcasted_iota(jnp.int32, (2 * nbd, LANES), 0)
    cb_at = lax.broadcasted_iota(jnp.int32, (cb, LANES), 0)

    def stacked(entries):
        out = jnp.zeros((len(entries), LANES), jnp.float32)
        for i, entry in enumerate(entries):
            out = jnp.where(tile_at == i, entry, out)
        return out

    col_peak = jnp.zeros((cb, LANES), jnp.float32)
    row_peaks = []
    for k in range(nbd):
        block = blocks_ref[k]
        flip = block.T
        flip_ref[k] = flip
        row_peaks.append(jnp.max(jnp.abs(flip), axis=0, keepdims=True))
        peak = jnp.max(jnp.abs(block), axis=0, keepdims=True)
        col_peak = jnp.maximum(col_peak, jnp.where(cb_at == cols[k], peak, 0.0))
    max_y[yi] = stacked(row_peaks + rows)
    cmax_buf[row] = col_peak
    pl.semaphore_wait(barrier, len(near))
    pl.semaphore_signal(reached, inc=1, device_id=col_device((1, 0, 0)), device_id_type=MESH)
    arrive = send(0, [col_device(d) for d in line_y], max_y, yi)
    arrive_c = send(1, [row_device(d) for d in line_r], cmax_buf, row)
    for copy in fetches[4:]:
        copy.wait()
    arrive()

    rb_at = lax.broadcasted_iota(jnp.int32, (rb, LANES), 0).astype(jnp.float32)
    lane = lax.broadcasted_iota(jnp.int32, (2 * nbd, LANES), 1)
    half = lane % (2 * nbd) // nbd
    mine = (lane // qlanes == lax.rem(qi, qper)) & (tile_at - nbd == lane % nbd)
    owner = lane % qlanes // (2 * nbd)
    dense = jnp.zeros((rb, LANES), jnp.float32)
    codes = jnp.zeros((2 * nbd, LANES), jnp.float32)
    for j in range(ny):
        for k in range(nbd):
            here = rb_at == max_y[j, nbd + k : nbd + k + 1]
            dense = jnp.maximum(dense, jnp.where(here, max_y[j, k : k + 1], 0.0))
        codes = jnp.where(mine & (owner == j), max_y[j], codes)
    codes = jnp.where(mine, codes + (half * rb).astype(jnp.float32), 0.0)
    max_q[qi, :rb] = dense
    max_q[qi, rb:] = jnp.broadcast_to(jnp.sum(codes, axis=0, keepdims=True), (8, LANES))
    pl.semaphore_wait(reached, 1)
    arrive = send(2, [col_device(d) for d in plane], max_q, qi)
    arrive_c()
    col_scale = 1.0 / jnp.sqrt(jnp.maximum(whole(cmax_buf, jnp.maximum), 0.5))
    cost_s = col_scale * cost_ref[...]
    upper_s = upper_ref[...] / col_scale
    x_prev = x_ref[...]
    eta = steps_ref[0]
    omega = steps_ref[1]
    omega_v = jnp.full((1, 1), omega)
    tau = eta / omega_v
    sigma = eta * omega
    arrive()
    rowmax = total([max_q[i, :rb] for i in range(nq)], jnp.maximum)
    row_scale = 1.0 / jnp.sqrt(jnp.maximum(rowmax, 0.5))
    scale_ref[...] = row_scale

    def backward(ref):
        got = [ref[pl.ds(brow[k], 1), :] * scale_ref[pl.ds(brow[k], 1), :] for k in range(nbd)]
        vec = stacked(got + got).T
        out = jnp.zeros((cb, LANES), jnp.float32)
        for k in range(nbd):
            prod = jnp.sum(blocks_ref[k] * vec[:, k : k + 1], axis=0, keepdims=True)
            out = out + jnp.where(cb_at == cols[k], prod, 0.0)
        return out

    part_buf[row] = backward(y_ref)
    arrive = send(3, [row_device(d) for d in line_r], part_buf, row)
    hot_at = lax.broadcasted_iota(jnp.int32, (2 * rb, LANES), 0).astype(jnp.float32)
    for g in range(nq // qper):
        code = total([max_q[i, rb : rb + 1] for i in range(g * qper, (g + 1) * qper)], jnp.add)
        hot_ref[:, g * LANES : (g + 1) * LANES] = jnp.where(hot_at == code, 1.0, 0.0).astype(jnp.bfloat16)
    rhs_s = row_scale * rhs_ref[...]
    arrive()
    grad = cost_s - whole(part_buf, jnp.add) * col_scale
    x_new = jnp.clip(x_prev - tau * grad, 0.0, upper_s)
    delta_x = x_new - x_prev
    vec_ref[0] = x_new * col_scale
    vec_ref[1] = delta_x * col_scale

    vecs = stacked([vec_ref[v, pl.ds(bcol[k], 1), :] for v in range(2) for k in range(nbd)]).T
    fwd_buf[slot] = stacked(
        [
            jnp.sum(flip_ref[k] * vecs[:, v * nbd + k : v * nbd + k + 1], axis=0, keepdims=True)
            for v in range(2)
            for k in range(nbd)
        ]
    )
    arrive = send(4, [col_device(d) for d in everyone], fwd_buf, slot)
    x_out[...] = x_new
    arrive()
    rest = fwd_buf[...].reshape(ncol * 2 * nbd, LANES)
    hot = hot_ref[...]
    pair = jnp.zeros((2 * rb, LANES), jnp.float32)
    for _ in range(3):
        part = rest.astype(jnp.bfloat16)
        rest = rest - part.astype(jnp.float32)
        pair = pair + jnp.dot(hot, part, preferred_element_type=jnp.float32)
    ax = pair[:rb] * row_scale
    adx = pair[rb:] * row_scale
    y_prev = y_ref[...]
    y_new = y_prev + sigma * (rhs_s - ax - adx)
    y_out[...] = y_new
    back_buf[row] = backward(y_out)
    arrive = send(5, [row_device(d) for d in line_r], back_buf, row)
    delta_y = y_new - y_prev
    resid = rhs_s - ax
    for at, term in enumerate((delta_y * delta_y, adx * adx, resid * resid, rhs_s * y_new)):
        dual_buf[row, at : at + 1] = jnp.sum(term, axis=0, keepdims=True)
    arrive_dual = send(6, [row_device(d) for d in line_r], dual_buf, row)

    def folded(term):
        out = jnp.sum(term, axis=0, keepdims=True)
        return out + pltpu.roll(out, LANES // 2, 1)

    moved = folded(delta_x * delta_x)
    left = lax.broadcasted_iota(jnp.int32, (1, LANES), 1) < LANES // 2
    arrive()
    reduced = cost_s - whole(back_buf, jnp.add) * col_scale
    sum_buf[slot] = jnp.where(left, moved, folded(cost_s * x_new + upper_s * jnp.maximum(-reduced, 0.0)))
    arrive = send(7, [mirror_device(d) for d in everyone], sum_buf, slot)
    arrive_dual()
    dual = jnp.sum(whole(dual_buf, jnp.add), axis=1, keepdims=True)
    dy2, adx2, res2, by = dual[0:1], dual[1:2], dual[2:3], dual[3:4]
    m = rb * LANES * nrow
    n = cb * LANES * ncol
    for copy in finish[:-1]:
        copy.wait()
    arrive()
    primal = whole(sum_buf, jnp.add)
    dx2 = jnp.sum(jnp.where(left, primal, 0.0), axis=1, keepdims=True)
    gain = jnp.sum(jnp.where(left, 0.0, primal), axis=1, keepdims=True)
    movement = 0.5 * omega * dx2 + 0.5 / omega_v * dy2
    at = lax.broadcasted_iota(jnp.int32, (1, LANES), 1)
    stats_out[...] = jnp.where(
        at == 0,
        jnp.sqrt(res2 / m),
        jnp.where(at == 1, (gain - by) / n, movement / jnp.sqrt(adx2 * dy2 + 1e-06)),
    )
    finish[-1].wait()


def shards(grid, nrow, blocks, block_rows, block_cols, counts, x_prev, y_prev, cost, rhs, upper, steps):
    nx, ny, nz = grid
    nbd, bsz = blocks.shape[2], blocks.shape[3]
    rb = y_prev.shape[0] // bsz
    cb = x_prev.shape[0] // bsz
    ncol = nx * ny * nz
    vmem = pl.BlockSpec(memory_space=pltpu.VMEM)
    hbm = pl.BlockSpec(memory_space=pl.ANY)
    f32 = jnp.float32

    def buf(*shape):
        return pltpu.VMEM((*shape, LANES), f32)

    x_new, y_new, stats = pl.pallas_call(
        functools.partial(body, grid, nrow, nbd),
        out_shape=(
            jax.ShapeDtypeStruct((cb, bsz), f32),
            jax.ShapeDtypeStruct((rb, bsz), f32),
            jax.ShapeDtypeStruct((1, LANES), f32),
        ),
        in_specs=[hbm] * 10,
        out_specs=(vmem, vmem, vmem),
        scratch_shapes=[
            pltpu.SMEM((1, 1, nbd), jnp.int32), pltpu.SMEM((1, 1, nbd), jnp.int32),
            pltpu.SMEM((1, 1), jnp.int32), pltpu.SMEM((2,), f32),
            buf(nbd, bsz), buf(cb), buf(rb), buf(cb), buf(rb), buf(cb),
            buf(nbd, bsz), buf(2, cb), buf(rb), pltpu.VMEM((2 * rb, ncol * 2 * nbd), jnp.bfloat16),
            buf(ny, 2 * nbd), buf(nx * nz, rb + 8), buf(nrow, cb), buf(nrow, cb), buf(ncol, 2 * nbd),
            buf(nrow, 4), buf(nrow, cb), buf(ncol, 1),
            pltpu.SemaphoreType.DMA((10,)),
            pltpu.SemaphoreType.DMA((8,)),
            pltpu.SemaphoreType.DMA((8,)),
            pltpu.SemaphoreType.REGULAR,
        ],
        compiler_params=pltpu.CompilerParams(collective_id=0, has_side_effects=True),
        name="pdlp",
    )(
        block_rows,
        block_cols,
        counts,
        steps,
        blocks.reshape(nbd, bsz, bsz),
        x_prev.reshape(cb, bsz),
        y_prev.reshape(rb, bsz),
        cost.reshape(cb, bsz),
        rhs.reshape(rb, bsz),
        upper.reshape(cb, bsz),
    )
    return x_new.reshape(-1), y_new.reshape(-1), stats[0, :3]


def solution(mesh):
    placed = (
        P("row", "col", None, None, None),
        P("row", "col", None),
        P("row", "col", None),
        P("row", "col"),
        P("col"),
        P("row"),
        P("col"),
        P("row"),
        P("col"),
        P(),
    )
    return jax.shard_map(
        functools.partial(shards, COL_GRID[mesh.shape["col"]], mesh.shape["row"]),
        mesh=mesh,
        in_specs=placed,
        out_specs=(P("col"), P("row"), P()),
        check_vma=False,
    )
```

time: 2340 us -> 75.7 us (0.03)
  the two profiles are of different devices: /device:TPU:8 before, /device:TPU:1 now
where the time goes in v2:
time: 75.7 us; the launch traced here: 74.5 us
  Pallas kernels  70.2 us (93%)
  local copies, waits for them, and re-layouts  3.03 us (4%)
  between operations  1.3 us (2%)
    pallas_call x1, Pallas kernels, shards(): pl.pallas_call(functools.partial(body, grid, nrow, nbd), out_shape=(jax.S...  70.2 us
    unnamed x4, local copies, waits for them, and re-layouts  1.88 us

profile of v2, /device:TPU:1, one launch (start us, length us, event | category | flops | bytes accessed | tf_op | source)
XLA Modules:
  0.0 74.5 jit_solution(4133213808392976753)
XLA Ops:
  1.3 70.2 %pdlp.1 = (f32[8,128]{1,0:T(8,128)}, f32[32,128]{1,0:T(8,128)}, f32[1,128]{1,0:T(1,128)}) custom-call(s32[1,1,4]{2,1,0:T(1,128)} %brow_hbm.1, s32[1,1,4]{2,1,0:T(1,128)} %bcol_hbm.1, s32[1,1]{1,0:T(1,128)S(6)} %copy.15.count_hbm, f32[2]{0:T(128)} %steps_hbm.1, f32[4,128,128]{2,1,0:T(8,128)} %bitcast.10, f32[8,128]{1,0:T(8,128)} %bitcast.14, ...), custom_call_target="tpu_custom_call" | custom-call | tf_op jit(solution)/shard_map/pdlp/pallas_call | solution.py:281
  71.5 0.0 copy-start
  71.5 1.2 %slice_bitcast_fusion = f32[3]{0:T(128)} fusion(f32[1,128]{1,0:T(1,128)} %get-tuple-element.8), kind=kLoop, calls=%fused_computation | loop fusion | bytes 24 | tf_op jit(solution)/shard_map/squeeze | solution.py:316
  72.7 1.3 %copy.16 = f32[1024]{0:T(1024)} copy(f32[1024]{0:T(1024)} %bitcast.17) | data formatting | bytes 8192
  73.9 0.0 copy-done
  73.9 0.6 copy.17
Async XLA Ops:
  71.5 2.4 %copy-start = (f32[32,128]{1,0:T(8,128)S(1)}, f32[32,128]{1,0:T(8,128)}, u32[]{:S(2)}) copy-start(f32[32,128]{1,0:T(8,128)} %get-tuple-element.7) | copy-start | bytes 49156

commit v3 on v2

--- a/solution.py
+++ b/solution.py
@@ -30,11 +30,11 @@
 
 def body(
     grid, nrow, nbd,
-    brow_hbm, bcol_hbm, count_hbm, steps_hbm, blocks_hbm, x_hbm, y_hbm, cost_hbm, rhs_hbm, upper_hbm,
+    brow_hbm, bcol_hbm, count_ref, steps_hbm, blocks_hbm, x_hbm, y_hbm, cost_hbm, rhs_hbm, upper_hbm,
     x_out, y_out, stats_out,
-    brow_ref, bcol_ref, count_ref, steps_ref, blocks_ref, x_ref, y_ref, cost_ref, rhs_ref, upper_ref,
+    brow_ref, bcol_ref, steps_ref, blocks_ref, x_ref, y_ref, cost_ref, rhs_ref, upper_ref,
     flip_ref, vec_ref, scale_ref, hot_ref,
-    max_y, max_q, cmax_buf, part_buf, fwd_buf, dual_buf, back_buf, sum_buf,
+    max_y, max_q, cmax_buf, part_buf, fwd_buf, move_buf, half_buf, term_buf, dual_buf, back_buf, sum_buf,
     local_sems, send_sems, recv_sems, reached,
 ):
     nx, ny, nz = grid
@@ -42,8 +42,8 @@
     cb = x_ref.shape[0]
     nq = nx * nz
     ncol = nq * ny
-    qlanes = ny * 2 * nbd
-    qper = LANES // qlanes
+    qlanes = ny * nbd
+    qper = min(LANES // qlanes, nq)
     row = lax.axis_index("row")
     col = lax.axis_index("col")
     xh = lax.div(col, ny * nz)
@@ -53,7 +53,6 @@
     ys = [lax.rem(yi + d, ny) for d in range(ny)]
     zs = [lax.rem(zi + d, nz) for d in range(nz)]
     rs = [lax.rem(row + d, nrow) for d in range(nrow)]
-    mirror = (nrow // 2 - 1 - lax.div(row, 2)) * 2 + lax.rem(row, 2)
     qi = xh * nz + zi
     slot = qi * ny + yi
 
@@ -61,11 +60,11 @@
         dx, dy, dz = d
         return (row, (xs[dx] * ny + ys[dy]) * nz + zs[dz])
 
-    def mirror_device(d):
-        return (mirror if d[0] else row, col_device(d)[1])
-
     def row_device(d):
         return (rs[d], col)
+
+    def ring_device(d):
+        return (rs[d[1]], col_device((d[0], 0, 0))[1])
 
     def ordered(offsets):
         cost = lambda d: (nx // 2) * 4 * d[0] + hops(d[1], ny) + hops(d[2], nz)
@@ -75,18 +74,19 @@
     line_z = [(0, 0, d) for d in far_first(nz)]
     plane = ordered([(a, 0, c) for a in range(nx) for c in range(nz) if a or c])
     everyone = ordered([(a, b, c) for a in range(nx) for b in range(ny) for c in range(nz) if a or b or c])
+    sheet = [d for d in everyone if not d[0]]
     line_r = far_first(nrow)
+    ring = [(a, d) for a in range(nx - 1, -1, -1) for d in far_first(nrow) + [0] * a]
+    partner = [col_device((1, 0, 0))]
 
     barrier = pltpu.get_barrier_semaphore()
     near = [col_device(d) for d in line_y] + [row_device(d) for d in line_r]
     near += [col_device(d) for d in line_z] + [col_device((1, 0, 0))]
-    for device in near:
-        pl.semaphore_signal(barrier, inc=1, device_id=device, device_id_type=MESH)
     fetches = [
         pltpu.make_async_copy(src, dst, local_sems.at[i])
         for i, (src, dst) in enumerate(
             (
-                (blocks_hbm, blocks_ref), (brow_hbm, brow_ref), (bcol_hbm, bcol_ref), (count_hbm, count_ref),
+                (blocks_hbm, blocks_ref), (brow_hbm, brow_ref), (bcol_hbm, bcol_ref),
                 (y_hbm, y_ref), (x_hbm, x_ref), (cost_hbm, cost_ref), (rhs_hbm, rhs_ref), (upper_hbm, upper_ref),
                 (steps_hbm, steps_ref),
             )
@@ -94,6 +94,8 @@
     ]
     for copy in fetches:
         copy.start()
+    for device in near:
+        pl.semaphore_signal(barrier, inc=1, device_id=device, device_id_type=MESH)
     finish = []
 
     def send(at, peers, buf, me):
@@ -113,7 +115,7 @@
     def whole(buf, op):
         return total([buf[i] for i in range(buf.shape[0])], op)
 
-    for copy in fetches[:4]:
+    for copy in fetches[:3]:
         copy.wait()
     count = count_ref[0, 0]
     brow = [brow_ref[0, 0, k] for k in range(nbd)]
@@ -144,15 +146,14 @@
     pl.semaphore_signal(reached, inc=1, device_id=col_device((1, 0, 0)), device_id_type=MESH)
     arrive = send(0, [col_device(d) for d in line_y], max_y, yi)
     arrive_c = send(1, [row_device(d) for d in line_r], cmax_buf, row)
-    for copy in fetches[4:]:
+    for copy in fetches[3:]:
         copy.wait()
     arrive()
 
     rb_at = lax.broadcasted_iota(jnp.int32, (rb, LANES), 0).astype(jnp.float32)
     lane = lax.broadcasted_iota(jnp.int32, (2 * nbd, LANES), 1)
-    half = lane % (2 * nbd) // nbd
     mine = (lane // qlanes == lax.rem(qi, qper)) & (tile_at - nbd == lane % nbd)
-    owner = lane % qlanes // (2 * nbd)
+    owner = lane % qlanes // nbd
     dense = jnp.zeros((rb, LANES), jnp.float32)
     codes = jnp.zeros((2 * nbd, LANES), jnp.float32)
     for j in range(ny):
@@ -160,7 +161,6 @@
             here = rb_at == max_y[j, nbd + k : nbd + k + 1]
             dense = jnp.maximum(dense, jnp.where(here, max_y[j, k : k + 1], 0.0))
         codes = jnp.where(mine & (owner == j), max_y[j], codes)
-    codes = jnp.where(mine, codes + (half * rb).astype(jnp.float32), 0.0)
     max_q[qi, :rb] = dense
     max_q[qi, rb:] = jnp.broadcast_to(jnp.sum(codes, axis=0, keepdims=True), (8, LANES))
     pl.semaphore_wait(reached, 1)
@@ -191,66 +191,85 @@
 
     part_buf[row] = backward(y_ref)
     arrive = send(3, [row_device(d) for d in line_r], part_buf, row)
-    hot_at = lax.broadcasted_iota(jnp.int32, (2 * rb, LANES), 0).astype(jnp.float32)
+    half_buf[xh, :cb] = cost_s
+    half_buf[xh, cb : 2 * cb] = upper_s
+    half_buf[xh, 2 * cb :] = col_scale
+    arrive_half = send(4, partner, half_buf, xh)
     for g in range(nq // qper):
         code = total([max_q[i, rb : rb + 1] for i in range(g * qper, (g + 1) * qper)], jnp.add)
-        hot_ref[:, g * LANES : (g + 1) * LANES] = jnp.where(hot_at == code, 1.0, 0.0).astype(jnp.bfloat16)
+        hot_ref[:, g * LANES : (g + 1) * LANES] = jnp.where(rb_at == code, 1.0, 0.0).astype(jnp.bfloat16)
     rhs_s = row_scale * rhs_ref[...]
     arrive()
     grad = cost_s - whole(part_buf, jnp.add) * col_scale
     x_new = jnp.clip(x_prev - tau * grad, 0.0, upper_s)
     delta_x = x_new - x_prev
-    vec_ref[0] = x_new * col_scale
+    vec_ref[0] = (x_new + delta_x) * col_scale
     vec_ref[1] = delta_x * col_scale
 
     vecs = stacked([vec_ref[v, pl.ds(bcol[k], 1), :] for v in range(2) for k in range(nbd)]).T
-    fwd_buf[slot] = stacked(
-        [
-            jnp.sum(flip_ref[k] * vecs[:, v * nbd + k : v * nbd + k + 1], axis=0, keepdims=True)
-            for v in range(2)
-            for k in range(nbd)
+
+    def forward(v):
+        prods = [
+            jnp.sum(flip_ref[k] * vecs[:, v * nbd + k : v * nbd + k + 1], axis=0, keepdims=True) for k in range(nbd)
         ]
-    )
-    arrive = send(4, [col_device(d) for d in everyone], fwd_buf, slot)
-    x_out[...] = x_new
-    arrive()
-    rest = fwd_buf[...].reshape(ncol * 2 * nbd, LANES)
-    hot = hot_ref[...]
-    pair = jnp.zeros((2 * rb, LANES), jnp.float32)
-    for _ in range(3):
-        part = rest.astype(jnp.bfloat16)
-        rest = rest - part.astype(jnp.float32)
-        pair = pair + jnp.dot(hot, part, preferred_element_type=jnp.float32)
-    ax = pair[:rb] * row_scale
-    adx = pair[rb:] * row_scale
-    y_prev = y_ref[...]
-    y_new = y_prev + sigma * (rhs_s - ax - adx)
-    y_out[...] = y_new
-    back_buf[row] = backward(y_out)
-    arrive = send(5, [row_device(d) for d in line_r], back_buf, row)
-    delta_y = y_new - y_prev
-    resid = rhs_s - ax
-    for at, term in enumerate((delta_y * delta_y, adx * adx, resid * resid, rhs_s * y_new)):
-        dual_buf[row, at : at + 1] = jnp.sum(term, axis=0, keepdims=True)
-    arrive_dual = send(6, [row_device(d) for d in line_r], dual_buf, row)
+        return stacked(prods + prods)[:nbd]
+
+    def gathered(ref):
+        rest = ref[...].reshape(ncol * nbd, LANES)
+        hot = hot_ref[:, : ncol * nbd]
+        out = jnp.zeros((rb, LANES), jnp.float32)
+        for _ in range(3):
+            part = rest.astype(jnp.bfloat16)
+            rest = rest - part.astype(jnp.float32)
+            out = out + jnp.dot(hot, part, preferred_element_type=jnp.float32)
+        return out * row_scale
 
     def folded(term):
         out = jnp.sum(term, axis=0, keepdims=True)
         return out + pltpu.roll(out, LANES // 2, 1)
 
-    moved = folded(delta_x * delta_x)
+    fwd_buf[slot] = forward(0)
+    arrive = send(5, [col_device(d) for d in everyone], fwd_buf, slot)
+    move_buf[slot] = forward(1)
+    arrive_move = send(6, [col_device(d) for d in everyone], move_buf, slot)
     left = lax.broadcasted_iota(jnp.int32, (1, LANES), 1) < LANES // 2
-    arrive()
-    reduced = cost_s - whole(back_buf, jnp.add) * col_scale
-    sum_buf[slot] = jnp.where(left, moved, folded(cost_s * x_new + upper_s * jnp.maximum(-reduced, 0.0)))
-    arrive = send(7, [mirror_device(d) for d in everyone], sum_buf, slot)
+    term_buf[xh] = jnp.where(left, folded(delta_x * delta_x), folded(cost_s * x_new))
+    arrive_term = send(7, partner, term_buf, xh)
+    x_out[...] = x_new
+    y_prev = y_ref[...]
+    arrive()
+    both = gathered(fwd_buf)
+    y_new = y_prev + sigma * (rhs_s - both)
+    y_out[...] = y_new
+    mine_at = xh * nrow + row
+    back_buf[mine_at] = backward(y_out)
+    arrive = send(8, [ring_device(d) for d in ring], back_buf, mine_at)
+    arrive_half()
+    arrive_term()
+    terms = total([term_buf[h] for h in range(nx)], jnp.add)
+    arrive()
+    gains = []
+    for h in range(nx):
+        product = total([back_buf[h * nrow + r] for r in range(nrow)], jnp.add)
+        reduced = half_buf[h, :cb] - product * half_buf[h, 2 * cb :]
+        gains.append(folded(half_buf[h, cb : 2 * cb] * jnp.maximum(-reduced, 0.0)))
+    spot = yi * nz + zi
+    sum_buf[spot] = terms + jnp.where(left, 0.0, total(gains, jnp.add))
+    arrive = send(9, [col_device(d) for d in sheet], sum_buf, spot)
+    arrive_move()
+    adx = gathered(move_buf)
+    delta_y = y_new - y_prev
+    resid = rhs_s - (both - adx)
+    for at, term in enumerate((delta_y * delta_y, adx * adx, resid * resid, rhs_s * y_new)):
+        dual_buf[row, at : at + 1] = jnp.sum(term, axis=0, keepdims=True)
+    arrive_dual = send(10, [row_device(d) for d in line_r], dual_buf, row)
+    for copy in finish[:-2]:
+        copy.wait()
     arrive_dual()
     dual = jnp.sum(whole(dual_buf, jnp.add), axis=1, keepdims=True)
     dy2, adx2, res2, by = dual[0:1], dual[1:2], dual[2:3], dual[3:4]
     m = rb * LANES * nrow
     n = cb * LANES * ncol
-    for copy in finish[:-1]:
-        copy.wait()
     arrive()
     primal = whole(sum_buf, jnp.add)
     dx2 = jnp.sum(jnp.where(left, primal, 0.0), axis=1, keepdims=True)
@@ -262,7 +281,14 @@
         jnp.sqrt(res2 / m),
         jnp.where(at == 1, (gain - by) / n, movement / jnp.sqrt(adx2 * dy2 + 1e-06)),
     )
-    finish[-1].wait()
+    for copy in finish[-2:]:
+        copy.wait()
+
+
+def publish(x_ref, y_ref, stats_ref, x_out, y_out, stats_out):
+    x_out[...] = x_ref[...]
+    y_out[...] = y_ref[...]
+    stats_out[...] = stats_ref[:, :3]
 
 
 def shards(grid, nrow, blocks, block_rows, block_cols, counts, x_prev, y_prev, cost, rhs, upper, steps):
@@ -272,7 +298,7 @@
     cb = x_prev.shape[0] // bsz
     ncol = nx * ny * nz
     vmem = pl.BlockSpec(memory_space=pltpu.VMEM)
-    hbm = pl.BlockSpec(memory_space=pl.ANY)
+    hbm = pl.BlockSpec(memory_space=pltpu.HBM)
     f32 = jnp.float32
 
     def buf(*shape):
@@ -281,22 +307,22 @@
     x_new, y_new, stats = pl.pallas_call(
         functools.partial(body, grid, nrow, nbd),
         out_shape=(
-            jax.ShapeDtypeStruct((cb, bsz), f32),
-            jax.ShapeDtypeStruct((rb, bsz), f32),
-            jax.ShapeDtypeStruct((1, LANES), f32),
+            pltpu.VMEM((cb, bsz), f32),
+            pltpu.VMEM((rb, bsz), f32),
+            pltpu.VMEM((1, LANES), f32),
         ),
-        in_specs=[hbm] * 10,
+        in_specs=[hbm] * 2 + [pl.BlockSpec(memory_space=pltpu.SMEM)] + [hbm] * 7,
         out_specs=(vmem, vmem, vmem),
         scratch_shapes=[
             pltpu.SMEM((1, 1, nbd), jnp.int32), pltpu.SMEM((1, 1, nbd), jnp.int32),
-            pltpu.SMEM((1, 1), jnp.int32), pltpu.SMEM((2,), f32),
+            pltpu.SMEM((2,), f32),
             buf(nbd, bsz), buf(cb), buf(rb), buf(cb), buf(rb), buf(cb),
-            buf(nbd, bsz), buf(2, cb), buf(rb), pltpu.VMEM((2 * rb, ncol * 2 * nbd), jnp.bfloat16),
-            buf(ny, 2 * nbd), buf(nx * nz, rb + 8), buf(nrow, cb), buf(nrow, cb), buf(ncol, 2 * nbd),
-            buf(nrow, 4), buf(nrow, cb), buf(ncol, 1),
-            pltpu.SemaphoreType.DMA((10,)),
-            pltpu.SemaphoreType.DMA((8,)),
-            pltpu.SemaphoreType.DMA((8,)),
+            buf(nbd, bsz), buf(2, cb), buf(rb), pltpu.VMEM((rb, max(ncol * nbd, LANES)), jnp.bfloat16),
+            buf(ny, 2 * nbd), buf(nx * nz, rb + 8), buf(nrow, cb), buf(nrow, cb), buf(ncol, nbd), buf(ncol, nbd),
+            buf(nx, 3 * cb), buf(nx, 1), buf(nrow, 4), buf(nx * nrow, cb), buf(ny * nz, 1),
+            pltpu.SemaphoreType.DMA((9,)),
+            pltpu.SemaphoreType.DMA((11,)),
+            pltpu.SemaphoreType.DMA((11,)),
             pltpu.SemaphoreType.REGULAR,
         ],
         compiler_params=pltpu.CompilerParams(collective_id=0, has_side_effects=True),
@@ -313,7 +339,18 @@
         rhs.reshape(rb, bsz),
         upper.reshape(cb, bsz),
     )
-    return x_new.reshape(-1), y_new.reshape(-1), stats[0, :3]
+    x_new, y_new, stats = pl.pallas_call(
+        publish,
+        out_shape=(
+            jax.ShapeDtypeStruct((cb, bsz), f32),
+            jax.ShapeDtypeStruct((rb, bsz), f32),
+            jax.ShapeDtypeStruct((1, 3), f32),
+        ),
+        in_specs=[vmem] * 3,
+        out_specs=(vmem,) * 3,
+        name="publish",
+    )(*(pltpu.with_memory_space_constraint(a, pltpu.VMEM) for a in (x_new, y_new, stats)))
+    return x_new.reshape(-1), y_new.reshape(-1), stats.reshape(-1)
 
 
 def solution(mesh):

time: 75.7 us -> 69.9 us (0.923); the launches traced: 74.5 us -> 69.7 us
  local copies, waits for them, and re-layouts: 3.03 us -> 0 us
  Pallas kernels: 70.2 us -> 68.4 us
    unnamed x4 -> x0, local copies, waits for them, and re-layouts: 1.88 us -> none
    pallas_call x1 -> x2, Pallas kernels: 70.2 us -> 68.4 us  [the longest x1 67.8 us: shards(): pl.pallas_call(functools.partial(body, grid, nrow, nbd), out_shape=(pltpu...]
    squeeze x1 -> x0, local copies, waits for them, and re-layouts: 1.15 us -> none  [shards(): return (x_new.reshape(-1), y_new.reshape(-1), stats[0, :3])]
where the time goes in v3:
time: 69.9 us; the launch traced here: 69.7 us
  Pallas kernels  68.4 us (98%)
  between operations  1.29 us (2%)
    pallas_call x1, Pallas kernels, shards(): pl.pallas_call(functools.partial(body, grid, nrow, nbd), out_shape=(pltpu...  67.8 us

profile of v3, /device:TPU:1, one launch (start us, length us, event | category | flops | bytes accessed | tf_op | source)
XLA Modules:
  0.0 69.7 jit_solution(3113728438946652496)
XLA Ops:
  1.3 67.8 %pdlp.1 = (f32[8,128]{1,0:T(8,128)S(1)}, f32[32,128]{1,0:T(8,128)S(1)}, f32[1,128]{1,0:T(1,128)S(1)}) custom-call(s32[1,1,4]{2,1,0:T(1,128)} %brow_hbm.1, s32[1,1,4]{2,1,0:T(1,128)} %bcol_hbm.1, s32[1,1]{1,0:T(1,128)S(6)} %copy.13.count_ref, f32[2]{0:T(128)} %steps_hbm.1, f32[4,128,128]{2,1,0:T(8,128)} %bitcast.9, f32[8,128]{1,0:T(8,128)} %bitcast.12, ...), custom_call_target="tpu_custom_call" | custom-call | tf_op jit(solution)/shard_map/pdlp/pallas_call | solution.py:307
  69.1 0.6 publish.1

commit v4 on v3

--- a/solution.py
+++ b/solution.py
@@ -34,7 +34,8 @@
     x_out, y_out, stats_out,
     brow_ref, bcol_ref, steps_ref, blocks_ref, x_ref, y_ref, cost_ref, rhs_ref, upper_ref,
     flip_ref, vec_ref, scale_ref, hot_ref,
-    max_y, max_q, cmax_buf, part_buf, fwd_buf, move_buf, half_buf, term_buf, dual_buf, back_buf, sum_buf,
+    max_y, max_q, code_q, cmax_buf, part_buf, fwd_buf, both_ref, move_send, move_y, move_q, half_buf, term_buf,
+    dual_buf, back_buf, sum_buf,
     local_sems, send_sems, recv_sems, reached,
 ):
     nx, ny, nz = grid
@@ -43,7 +44,10 @@
     nq = nx * nz
     ncol = nq * ny
     qlanes = ny * nbd
-    qper = min(LANES // qlanes, nq)
+    qper = min(LANES // qlanes, nz)
+    width = qper * qlanes
+    half = ny * nz
+    share = rb // ny
     row = lax.axis_index("row")
     col = lax.axis_index("col")
     xh = lax.div(col, ny * nz)
@@ -63,6 +67,9 @@
     def row_device(d):
         return (rs[d], col)
 
+    def table_device(d):
+        return (rs[d[1]], col_device((0, d[0], 0))[1])
+
     def ring_device(d):
         return (rs[d[1]], col_device((d[0], 0, 0))[1])
 
@@ -75,9 +82,11 @@
     plane = ordered([(a, 0, c) for a in range(nx) for c in range(nz) if a or c])
     everyone = ordered([(a, b, c) for a in range(nx) for b in range(ny) for c in range(nz) if a or b or c])
     sheet = [d for d in everyone if not d[0]]
+    beyond = [d for d in everyone if d[0]]
     line_r = far_first(nrow)
     ring = [(a, d) for a in range(nx - 1, -1, -1) for d in far_first(nrow) + [0] * a]
     partner = [col_device((1, 0, 0))]
+    table = [(b, d) for b in far_first(ny) + [0] for d in far_first(nrow) + [0] if b or d]
 
     barrier = pltpu.get_barrier_semaphore()
     near = [col_device(d) for d in line_y] + [row_device(d) for d in line_r]
@@ -98,10 +107,10 @@
         pl.semaphore_signal(barrier, inc=1, device_id=device, device_id_type=MESH)
     finish = []
 
-    def send(at, peers, buf, me):
-        for device in peers:
+    def send(at, peers, buf, me, sources=None):
+        for i, device in enumerate(peers):
             pltpu.make_async_remote_copy(
-                src_ref=buf.at[me],
+                src_ref=sources[i] if sources else buf.at[me],
                 dst_ref=buf.at[me],
                 send_sem=send_sems.at[at],
                 recv_sem=recv_sems.at[at],
@@ -148,23 +157,24 @@
     arrive_c = send(1, [row_device(d) for d in line_r], cmax_buf, row)
     for copy in fetches[3:]:
         copy.wait()
-    arrive()
-
     rb_at = lax.broadcasted_iota(jnp.int32, (rb, LANES), 0).astype(jnp.float32)
     lane = lax.broadcasted_iota(jnp.int32, (2 * nbd, LANES), 1)
     mine = (lane // qlanes == lax.rem(qi, qper)) & (tile_at - nbd == lane % nbd)
     owner = lane % qlanes // nbd
+    arrive()
     dense = jnp.zeros((rb, LANES), jnp.float32)
-    codes = jnp.zeros((2 * nbd, LANES), jnp.float32)
     for j in range(ny):
         for k in range(nbd):
             here = rb_at == max_y[j, nbd + k : nbd + k + 1]
             dense = jnp.maximum(dense, jnp.where(here, max_y[j, k : k + 1], 0.0))
-        codes = jnp.where(mine & (owner == j), max_y[j], codes)
-    max_q[qi, :rb] = dense
-    max_q[qi, rb:] = jnp.broadcast_to(jnp.sum(codes, axis=0, keepdims=True), (8, LANES))
+    max_q[qi] = dense
     pl.semaphore_wait(reached, 1)
     arrive = send(2, [col_device(d) for d in plane], max_q, qi)
+    codes = jnp.zeros((2 * nbd, LANES), jnp.float32)
+    for j in range(ny):
+        codes = jnp.where(mine & (owner == j), max_y[j], codes)
+    code_q[qi] = jnp.sum(codes, axis=0, keepdims=True)
+    arrive_code = send(3, [col_device(d) for d in plane], code_q, qi)
     arrive_c()
     col_scale = 1.0 / jnp.sqrt(jnp.maximum(whole(cmax_buf, jnp.maximum), 0.5))
     cost_s = col_scale * cost_ref[...]
@@ -176,7 +186,7 @@
     tau = eta / omega_v
     sigma = eta * omega
     arrive()
-    rowmax = total([max_q[i, :rb] for i in range(nq)], jnp.maximum)
+    rowmax = whole(max_q, jnp.maximum)
     row_scale = 1.0 / jnp.sqrt(jnp.maximum(rowmax, 0.5))
     scale_ref[...] = row_scale
 
@@ -190,14 +200,16 @@
         return out
 
     part_buf[row] = backward(y_ref)
-    arrive = send(3, [row_device(d) for d in line_r], part_buf, row)
+    arrive = send(12, [row_device(d) for d in line_r], part_buf, row)
     half_buf[xh, :cb] = cost_s
     half_buf[xh, cb : 2 * cb] = upper_s
     half_buf[xh, 2 * cb :] = col_scale
     arrive_half = send(4, partner, half_buf, xh)
+    arrive_code()
     for g in range(nq // qper):
-        code = total([max_q[i, rb : rb + 1] for i in range(g * qper, (g + 1) * qper)], jnp.add)
-        hot_ref[:, g * LANES : (g + 1) * LANES] = jnp.where(rb_at == code, 1.0, 0.0).astype(jnp.bfloat16)
+        code = total([code_q[i] for i in range(g * qper, (g + 1) * qper)], jnp.add)
+        h, start = divmod(g * width, half * nbd)
+        hot_ref[h, :, start : start + width] = jnp.where(rb_at == code, 1.0, 0.0).astype(jnp.bfloat16)[:, :width]
     rhs_s = row_scale * rhs_ref[...]
     arrive()
     grad = cost_s - whole(part_buf, jnp.add) * col_scale
@@ -209,41 +221,67 @@
     vecs = stacked([vec_ref[v, pl.ds(bcol[k], 1), :] for v in range(2) for k in range(nbd)]).T
 
     def forward(v):
-        prods = [
+        return [
             jnp.sum(flip_ref[k] * vecs[:, v * nbd + k : v * nbd + k + 1], axis=0, keepdims=True) for k in range(nbd)
         ]
-        return stacked(prods + prods)[:nbd]
-
-    def gathered(ref):
-        rest = ref[...].reshape(ncol * nbd, LANES)
-        hot = hot_ref[:, : ncol * nbd]
+
+    def gathered(ref, h):
+        rest = ref[pl.ds(h * half, half)].reshape(half * nbd, LANES)
+        hot = hot_ref[h]
         out = jnp.zeros((rb, LANES), jnp.float32)
         for _ in range(3):
             part = rest.astype(jnp.bfloat16)
             rest = rest - part.astype(jnp.float32)
             out = out + jnp.dot(hot, part, preferred_element_type=jnp.float32)
-        return out * row_scale
+        return out
 
     def folded(term):
         out = jnp.sum(term, axis=0, keepdims=True)
         return out + pltpu.roll(out, LANES // 2, 1)
 
-    fwd_buf[slot] = forward(0)
-    arrive = send(5, [col_device(d) for d in everyone], fwd_buf, slot)
-    move_buf[slot] = forward(1)
-    arrive_move = send(6, [col_device(d) for d in everyone], move_buf, slot)
+    prods = forward(0)
+    fwd_buf[slot] = stacked(prods + prods)[:nbd]
+    arrive_far = send(5, [col_device(d) for d in beyond], fwd_buf, slot)
+    prods = forward(1)
+    share_at = lax.broadcasted_iota(jnp.int32, (share, LANES), 0).astype(jnp.float32)
+    for j in range(ny):
+        move_send[j] = total([jnp.where(share_at + j * share == rows[k], prods[k], 0.0) for k in range(nbd)], jnp.add)
+    move_y[yi] = move_send[yi]
+    arrive_move = send(6, [col_device(d) for d in line_y], move_y, yi, [move_send.at[ys[d[1]]] for d in line_y])
+    arrive = send(11, [col_device(d) for d in sheet], fwd_buf, slot)
     left = lax.broadcasted_iota(jnp.int32, (1, LANES), 1) < LANES // 2
     term_buf[xh] = jnp.where(left, folded(delta_x * delta_x), folded(cost_s * x_new))
     arrive_term = send(7, partner, term_buf, xh)
     x_out[...] = x_new
     y_prev = y_ref[...]
-    arrive()
-    both = gathered(fwd_buf)
+    arrive_move()
+    move_q[qi] = whole(move_y, jnp.add)
+    arrive_move = send(13, [col_device(d) for d in plane], move_q, qi)
+    arrive()
+    both = gathered(fwd_buf, xh)
+    arrive_far()
+    both = (both + gathered(fwd_buf, 1 - xh)) * row_scale
+    both_ref[...] = rhs_s - both
     y_new = y_prev + sigma * (rhs_s - both)
     y_out[...] = y_new
     mine_at = xh * nrow + row
     back_buf[mine_at] = backward(y_out)
     arrive = send(8, [ring_device(d) for d in ring], back_buf, mine_at)
+    arrive_move()
+    at = pl.ds(pl.multiple_of(yi * share, share), share)
+    scale = scale_ref[at, :]
+    adx = whole(move_q, jnp.add) * scale
+    y_share = y_out[at, :]
+    delta_y = y_share - y_ref[at, :]
+    resid = both_ref[at, :] + adx
+    quarter = lax.broadcasted_iota(jnp.int32, (1, LANES), 1) // (LANES // 4)
+    duals = jnp.zeros((1, LANES), jnp.float32)
+    for i, term in enumerate((delta_y * delta_y, adx * adx, resid * resid, scale * rhs_ref[at, :] * y_share)):
+        term = folded(term)
+        duals = jnp.where(quarter == i, term + pltpu.roll(term, LANES // 4, 1), duals)
+    spot = yi * nrow + row
+    dual_buf[spot] = duals
+    arrive_dual = send(10, [table_device(d) for d in table], dual_buf, spot)
     arrive_half()
     arrive_term()
     terms = total([term_buf[h] for h in range(nx)], jnp.add)
@@ -256,18 +294,11 @@
     spot = yi * nz + zi
     sum_buf[spot] = terms + jnp.where(left, 0.0, total(gains, jnp.add))
     arrive = send(9, [col_device(d) for d in sheet], sum_buf, spot)
-    arrive_move()
-    adx = gathered(move_buf)
-    delta_y = y_new - y_prev
-    resid = rhs_s - (both - adx)
-    for at, term in enumerate((delta_y * delta_y, adx * adx, resid * resid, rhs_s * y_new)):
-        dual_buf[row, at : at + 1] = jnp.sum(term, axis=0, keepdims=True)
-    arrive_dual = send(10, [row_device(d) for d in line_r], dual_buf, row)
-    for copy in finish[:-2]:
+    for copy in finish[:-1]:
         copy.wait()
     arrive_dual()
-    dual = jnp.sum(whole(dual_buf, jnp.add), axis=1, keepdims=True)
-    dy2, adx2, res2, by = dual[0:1], dual[1:2], dual[2:3], dual[3:4]
+    dual = whole(dual_buf, jnp.add)
+    dy2, adx2, res2, by = (jnp.sum(jnp.where(quarter == i, dual, 0.0), axis=1, keepdims=True) for i in range(4))
     m = rb * LANES * nrow
     n = cb * LANES * ncol
     arrive()
@@ -281,8 +312,7 @@
         jnp.sqrt(res2 / m),
         jnp.where(at == 1, (gain - by) / n, movement / jnp.sqrt(adx2 * dy2 + 1e-06)),
     )
-    for copy in finish[-2:]:
-        copy.wait()
+    finish[-1].wait()
 
 
 def publish(x_ref, y_ref, stats_ref, x_out, y_out, stats_out):
@@ -317,12 +347,12 @@
             pltpu.SMEM((1, 1, nbd), jnp.int32), pltpu.SMEM((1, 1, nbd), jnp.int32),
             pltpu.SMEM((2,), f32),
             buf(nbd, bsz), buf(cb), buf(rb), buf(cb), buf(rb), buf(cb),
-            buf(nbd, bsz), buf(2, cb), buf(rb), pltpu.VMEM((rb, max(ncol * nbd, LANES)), jnp.bfloat16),
-            buf(ny, 2 * nbd), buf(nx * nz, rb + 8), buf(nrow, cb), buf(nrow, cb), buf(ncol, nbd), buf(ncol, nbd),
-            buf(nx, 3 * cb), buf(nx, 1), buf(nrow, 4), buf(nx * nrow, cb), buf(ny * nz, 1),
+            buf(nbd, bsz), buf(2, cb), buf(rb), pltpu.VMEM((nx, rb, ny * nz * nbd), jnp.bfloat16),
+            buf(ny, 2 * nbd), buf(nx * nz, rb), buf(nx * nz, 1), buf(nrow, cb), buf(nrow, cb), buf(ncol, nbd), buf(rb),
+            buf(ny, rb // ny), buf(ny, rb // ny), buf(nx * nz, rb // ny), buf(nx, 3 * cb), buf(nx, 1), buf(ny * nrow, 1), buf(nx * nrow, cb), buf(ny * nz, 1),
             pltpu.SemaphoreType.DMA((9,)),
-            pltpu.SemaphoreType.DMA((11,)),
-            pltpu.SemaphoreType.DMA((11,)),
+            pltpu.SemaphoreType.DMA((14,)),
+            pltpu.SemaphoreType.DMA((14,)),
             pltpu.SemaphoreType.REGULAR,
         ],
         compiler_params=pltpu.CompilerParams(collective_id=0, has_side_effects=True),

time: 69.9 us -> 66.3 us (0.948)
  Pallas kernels: 68.4 us -> 64.8 us
    pallas_call x1, Pallas kernels: 67.8 us -> 64.2 us  [shards(): pl.pallas_call(functools.partial(body, grid, nrow, nbd), out_shape=(pltpu...]
where the time goes in v4:
time: 66.3 us; the launch traced here: 66.1 us
  Pallas kernels  64.8 us (98%)
  between operations  1.29 us (2%)
    pallas_call x1, Pallas kernels, shards(): pl.pallas_call(functools.partial(body, grid, nrow, nbd), out_shape=(pltpu...  64.2 us

profile of v4, /device:TPU:1, one launch (start us, length us, event | category | flops | bytes accessed | tf_op | source)
XLA Modules:
  0.0 66.1 jit_solution(3601907115369149842)
XLA Ops:
  1.3 64.2 %pdlp.1 = (f32[8,128]{1,0:T(8,128)S(1)}, f32[32,128]{1,0:T(8,128)S(1)}, f32[1,128]{1,0:T(1,128)S(1)}) custom-call(s32[1,1,4]{2,1,0:T(1,128)} %brow_hbm.1, s32[1,1,4]{2,1,0:T(1,128)} %bcol_hbm.1, s32[1,1]{1,0:T(1,128)S(6)} %copy.13.count_ref, f32[2]{0:T(128)} %steps_hbm.1, f32[4,128,128]{2,1,0:T(8,128)} %bitcast.9, f32[8,128]{1,0:T(8,128)} %bitcast.12, ...), custom_call_target="tpu_custom_call" | custom-call | tf_op jit(solution)/shard_map/pdlp/pallas_call | solution.py:337
  65.5 0.6 publish.1

commit v5 on v4

--- a/solution.py
+++ b/solution.py
@@ -32,15 +32,15 @@
     grid, nrow, nbd,
     brow_hbm, bcol_hbm, count_ref, steps_hbm, blocks_hbm, x_hbm, y_hbm, cost_hbm, rhs_hbm, upper_hbm,
     x_out, y_out, stats_out,
-    brow_ref, bcol_ref, steps_ref, blocks_ref, x_ref, y_ref, cost_ref, rhs_ref, upper_ref,
+    brow_ref, bcol_ref, steps_ref, blocks_ref, vectors,
     flip_ref, vec_ref, scale_ref, hot_ref,
     max_y, max_q, code_q, cmax_buf, part_buf, fwd_buf, both_ref, move_send, move_y, move_q, half_buf, term_buf,
     dual_buf, back_buf, sum_buf,
     local_sems, send_sems, recv_sems, reached,
 ):
     nx, ny, nz = grid
-    rb = y_ref.shape[0]
-    cb = x_ref.shape[0]
+    rb = y_hbm.shape[0]
+    cb = x_hbm.shape[0]
     nq = nx * nz
     ncol = nq * ny
     qlanes = ny * nbd
@@ -57,6 +57,11 @@
     ys = [lax.rem(yi + d, ny) for d in range(ny)]
     zs = [lax.rem(zi + d, nz) for d in range(nz)]
     rs = [lax.rem(row + d, nrow) for d in range(nrow)]
+    place, core = lax.div(row, 2), lax.rem(row, 2)
+    chips = [place]
+    if nrow == 8:
+        chips = [3 - place, lax.rem(place + 2, 4), place + 1 - 2 * lax.rem(place, 2), place]
+    homes = [(chip * 2 + core, chip * 2 + 1 - core) for chip in chips]
     qi = xh * nz + zi
     slot = qi * ny + yi
 
@@ -64,14 +69,8 @@
         dx, dy, dz = d
         return (row, (xs[dx] * ny + ys[dy]) * nz + zs[dz])
 
-    def row_device(d):
-        return (rs[d], col)
-
     def table_device(d):
         return (rs[d[1]], col_device((0, d[0], 0))[1])
-
-    def ring_device(d):
-        return (rs[d[1]], col_device((d[0], 0, 0))[1])
 
     def ordered(offsets):
         cost = lambda d: (nx // 2) * 4 * d[0] + hops(d[1], ny) + hops(d[2], nz)
@@ -83,24 +82,31 @@
     everyone = ordered([(a, b, c) for a in range(nx) for b in range(ny) for c in range(nz) if a or b or c])
     sheet = [d for d in everyone if not d[0]]
     beyond = [d for d in everyone if d[0]]
-    line_r = far_first(nrow)
-    ring = [(a, d) for a in range(nx - 1, -1, -1) for d in far_first(nrow) + [0] * a]
+    beside = col_device((1, 0, 0))[1]
+    line_r = [(home, col) for pair in homes[:-1] for home in pair] + [(homes[-1][1], col)]
+    ring = [(home, beside) for pair in homes[::-1] for home in pair]
+    split = len(ring) // 2
+    ring = ring[:split] + line_r[: split // 2] + ring[split:] + line_r[split // 2 :]
     partner = [col_device((1, 0, 0))]
     table = [(b, d) for b in far_first(ny) + [0] for d in far_first(nrow) + [0] if b or d]
 
     barrier = pltpu.get_barrier_semaphore()
-    near = [col_device(d) for d in line_y] + [row_device(d) for d in line_r]
+    near = [col_device(d) for d in line_y] + line_r
     near += [col_device(d) for d in line_z] + [col_device((1, 0, 0))]
+    lines = [(x_hbm, cb), (cost_hbm, cb), (upper_hbm, cb), (y_hbm, rb), (rhs_hbm, rb)]
+    starts = [sum(n for _, n in lines[:i]) for i in range(len(lines))]
+    x_ref, cost_ref, upper_ref, y_ref, rhs_ref = (
+        vectors.at[pl.ds(start, n)] for start, (_, n) in zip(starts, lines)
+    )
     fetches = [
-        pltpu.make_async_copy(src, dst, local_sems.at[i])
-        for i, (src, dst) in enumerate(
-            (
-                (blocks_hbm, blocks_ref), (brow_hbm, brow_ref), (bcol_hbm, bcol_ref),
-                (y_hbm, y_ref), (x_hbm, x_ref), (cost_hbm, cost_ref), (rhs_hbm, rhs_ref), (upper_hbm, upper_ref),
-                (steps_hbm, steps_ref),
-            )
-        )
+        pltpu.make_async_copy(blocks_hbm, blocks_ref, local_sems.at[0]),
+        pltpu.make_async_copy(brow_hbm, brow_ref, local_sems.at[1]),
+        pltpu.make_async_copy(bcol_hbm, bcol_ref, local_sems.at[2]),
+        pltpu.make_async_copy(steps_hbm, steps_ref, local_sems.at[3]),
     ]
+    for (src, _), dst in zip(lines, (x_ref, cost_ref, upper_ref, y_ref, rhs_ref)):
+        pltpu.make_async_copy(src, dst, local_sems.at[4]).start()
+    late = [fetches[3], pltpu.make_async_copy(vectors, vectors, local_sems.at[4])]
     for copy in fetches:
         copy.start()
     for device in near:
@@ -154,8 +160,8 @@
     pl.semaphore_wait(barrier, len(near))
     pl.semaphore_signal(reached, inc=1, device_id=col_device((1, 0, 0)), device_id_type=MESH)
     arrive = send(0, [col_device(d) for d in line_y], max_y, yi)
-    arrive_c = send(1, [row_device(d) for d in line_r], cmax_buf, row)
-    for copy in fetches[3:]:
+    arrive_c = send(1, line_r, cmax_buf, row)
+    for copy in late:
         copy.wait()
     rb_at = lax.broadcasted_iota(jnp.int32, (rb, LANES), 0).astype(jnp.float32)
     lane = lax.broadcasted_iota(jnp.int32, (2 * nbd, LANES), 1)
@@ -200,7 +206,7 @@
         return out
 
     part_buf[row] = backward(y_ref)
-    arrive = send(12, [row_device(d) for d in line_r], part_buf, row)
+    arrive = send(12, line_r, part_buf, row)
     half_buf[xh, :cb] = cost_s
     half_buf[xh, cb : 2 * cb] = upper_s
     half_buf[xh, 2 * cb :] = col_scale
@@ -266,7 +272,7 @@
     y_out[...] = y_new
     mine_at = xh * nrow + row
     back_buf[mine_at] = backward(y_out)
-    arrive = send(8, [ring_device(d) for d in ring], back_buf, mine_at)
+    arrive = send(8, ring, back_buf, mine_at)
     arrive_move()
     at = pl.ds(pl.multiple_of(yi * share, share), share)
     scale = scale_ref[at, :]
@@ -346,11 +352,11 @@
         scratch_shapes=[
             pltpu.SMEM((1, 1, nbd), jnp.int32), pltpu.SMEM((1, 1, nbd), jnp.int32),
             pltpu.SMEM((2,), f32),
-            buf(nbd, bsz), buf(cb), buf(rb), buf(cb), buf(rb), buf(cb),
+            buf(nbd, bsz), buf(3 * cb + 2 * rb),
             buf(nbd, bsz), buf(2, cb), buf(rb), pltpu.VMEM((nx, rb, ny * nz * nbd), jnp.bfloat16),
             buf(ny, 2 * nbd), buf(nx * nz, rb), buf(nx * nz, 1), buf(nrow, cb), buf(nrow, cb), buf(ncol, nbd), buf(rb),
             buf(ny, rb // ny), buf(ny, rb // ny), buf(nx * nz, rb // ny), buf(nx, 3 * cb), buf(nx, 1), buf(ny * nrow, 1), buf(nx * nrow, cb), buf(ny * nz, 1),
-            pltpu.SemaphoreType.DMA((9,)),
+            pltpu.SemaphoreType.DMA((5,)),
             pltpu.SemaphoreType.DMA((14,)),
             pltpu.SemaphoreType.DMA((14,)),
             pltpu.SemaphoreType.REGULAR,

time: 66.3 us -> 66 us (level)
  no operation moved by 1% of the time
where the time goes in v5:
time: 66 us; the launch traced here: 65.9 us
  Pallas kernels  64.6 us (98%)
  between operations  1.29 us (2%)
    pallas_call x1, Pallas kernels, shards(): pl.pallas_call(functools.partial(body, grid, nrow, nbd), out_shape=(pltpu...  64 us

profile of v5, /device:TPU:1, one launch (start us, length us, event | category | flops | bytes accessed | tf_op | source)
XLA Modules:
  0.0 65.9 jit_solution(4188571717549432399)
XLA Ops:
  1.3 64.0 %pdlp.1 = (f32[8,128]{1,0:T(8,128)S(1)}, f32[32,128]{1,0:T(8,128)S(1)}, f32[1,128]{1,0:T(1,128)S(1)}) custom-call(s32[1,1,4]{2,1,0:T(1,128)} %brow_hbm.1, s32[1,1,4]{2,1,0:T(1,128)} %bcol_hbm.1, s32[1,1]{1,0:T(1,128)S(6)} %copy.13.count_ref, f32[2]{0:T(128)} %steps_hbm.1, f32[4,128,128]{2,1,0:T(8,128)} %bitcast.9, f32[8,128]{1,0:T(8,128)} %bitcast.12, ...), custom_call_target="tpu_custom_call" | custom-call | tf_op jit(solution)/shard_map/pdlp/pallas_call | solution.py:343
  65.3 0.6 publish.1
